TPU v7x, 32 devices: a whole 2x2x4 slice. The times are simulated.
32 devices in a mesh: dp: 4 (over y, x), fsdp: 4 (over z), crop: 2 (over core).
Axes of the slice: x: 2, y: 2, z: 4, core: 2. Of those that a mesh axis runs over, the one named last changes fastest.
Arguments:
- grad_parts: float32 [8, 848, 1536], P(('dp', 'crop'), None, 'fsdp'), may hold values from -1.5 to 1.5
- student: float32 [848, 1536], P(('dp', 'crop'), 'fsdp'), may hold values from -2 to 2
- teacher: float32 [848, 1536], P(('dp', 'crop'), 'fsdp'), may hold values from -2 to 2
- moment1: float32 [848, 1536], P(('dp', 'crop'), 'fsdp'), may hold values from -0.6 to 0.6
- moment2: float32 [848, 1536], P(('dp', 'crop'), 'fsdp'), may hold values from 0.001 to 0.01
- step_count: int32 [1], replicated, may hold values from 1 to 1999
- pixels: bfloat16 [16, 2, 256, 588], P(('dp', 'fsdp'), 'crop'), may hold values from -5 to 5
- assign: int32 [16, 2], P(('dp', 'fsdp')), may hold values from 0 to 1, each once within a row
Outputs:
- student_new: float32 [848, 1536], P(('dp', 'crop'), 'fsdp')
- moment1_new: float32 [848, 1536], P(('dp', 'crop'), 'fsdp')
- moment2_new: float32 [848, 1536], P(('dp', 'crop'), 'fsdp')
- teacher_new: float32 [848, 1536], P(('dp', 'crop'), 'fsdp')
- student_step: float32 [848, 1536], P(('dp', 'crop'), 'fsdp')
- teacher_tokens: float32 [16, 2, 257, 1536], P(('dp', 'fsdp'))
Inputs may be any that keep to these rules, and one draw needn't show every extreme that they name: `assign`: each row holds 0 and 1 once.
All inputs are finite; a program needn't handle non-finite values.
Results may differ from a plain program's by a relative error of at most 0.0003.
Values may be sent and summed in bfloat16 or wider, within the bound.
A program may use at most 64 MiB of HBM per device.

v0:
```python
import math
import jax
import jax.numpy as jnp
from jax import lax
from jax.sharding import PartitionSpec as P

beta_one = 0.9
beta_two = 0.999
adam_epsilon = 1e-08
learn_rate = 0.001
weight_decay = 0.04
momentum_base = 0.992
plan_length = 625000.0
norm_epsilon = 1e-06


def optimize(gradient, student, teacher, moment1, moment2, step_count):
    step_value = step_count[0].astype(jnp.float32)
    first_moment = beta_one * moment1 + (1.0 - beta_one) * gradient
    second_moment = beta_two * moment2 + (1.0 - beta_two) * gradient * gradient
    first_fix = 1.0 - jnp.power(jnp.float32(beta_one), step_value)
    second_fix = 1.0 - jnp.power(jnp.float32(beta_two), step_value)
    update = (
        first_moment / first_fix / (jnp.sqrt(second_moment / second_fix) + adam_epsilon)
        + weight_decay * student
    )
    student_new = student - learn_rate * update
    momentum = (
        1.0 - (1.0 - momentum_base) * (jnp.cos(math.pi * step_value / plan_length) + 1.0) / 2.0
    )
    teacher_new = momentum * teacher + (1.0 - momentum) * student_new
    return (student_new, first_moment, second_moment, teacher_new, update)


def embed(patches, table):
    count = patches.shape[0]
    pix_size = patches.shape[2]
    patch_count = patches.shape[1]
    width = table.shape[1]
    weight = table[:pix_size]
    position = table[pix_size : pix_size + patch_count]
    extras = table[pix_size + patch_count :]
    flat_patches = patches.reshape(count * patch_count, pix_size).astype(jnp.float32)
    projected = jnp.dot(
        flat_patches, weight, precision=lax.Precision.HIGHEST, preferred_element_type=jnp.float32
    )
    projected = projected.reshape(count, patch_count, width) + extras[1] + position
    class_row = jnp.broadcast_to(extras[0], (count, 1, width))
    tokens = jnp.concatenate([class_row, projected], axis=1)
    average = jnp.mean(tokens, axis=-1, keepdims=True)
    centered = tokens - average
    variance = jnp.mean(centered * centered, axis=-1, keepdims=True)
    return centered * lax.rsqrt(variance + norm_epsilon) * extras[2] + extras[3]


def shards(grad_parts, student, teacher, moment1, moment2, step_count, pixels, assign):
    gradient = lax.psum_scatter(grad_parts[0], ("dp", "crop"), scatter_dimension=0, tiled=True)
    student_new, first_moment, second_moment, teacher_new, update = optimize(
        gradient, student, teacher, moment1, moment2, step_count
    )
    column_block = lax.all_gather(teacher_new, "fsdp", axis=1, tiled=True)
    gathered = lax.all_gather(column_block, ("dp", "crop"), axis=0, tiled=True)
    own_tokens = embed(pixels[:, 0], gathered)
    both = lax.all_gather(own_tokens[:, None], "crop", axis=1, tiled=True)
    teacher_tokens = jnp.where((assign == 0)[:, :, None, None], both[:, 0:1], both[:, 1:2])
    return (student_new, first_moment, second_moment, teacher_new, update, teacher_tokens)


def solution(mesh):
    placed = (
        P(("dp", "crop"), None, "fsdp"),
        P(("dp", "crop"), "fsdp"),
        P(("dp", "crop"), "fsdp"),
        P(("dp", "crop"), "fsdp"),
        P(("dp", "crop"), "fsdp"),
        P(),
        P(("dp", "fsdp"), "crop", None, None),
        P(("dp", "fsdp"), None),
    )
    return jax.shard_map(
        shards,
        mesh=mesh,
        in_specs=placed,
        out_specs=(
            P(("dp", "crop"), "fsdp"),
            P(("dp", "crop"), "fsdp"),
            P(("dp", "crop"), "fsdp"),
            P(("dp", "crop"), "fsdp"),
            P(("dp", "crop"), "fsdp"),
            P(("dp", "fsdp"), None, None, None),
        ),
        check_vma=False,
    )
```

profile of v0, /device:TPU:0, one launch (start us, length us, event | category | flops | bytes accessed | tf_op | source)
XLA Modules:
  0.0 138.0 jit_solution(8425231990737697508)
XLA Ops:
  7.2 0.0 copy-start
  7.2 0.0 copy-start.6
  7.2 0.0 all-gather.6.cloned.1.call-start
  7.3 23.7 %fusion = f32[112,384]{1,0:T(8,128)S(1)} fusion(f32[848,384]{1,0:T(8,128)} %bitcast.31), kind=kCustom, calls=%all-reduce-scatter | all-reduce-scatter fusion | flops 344065 | bytes 1475072
  31.0 1.3 collective-permute-start
  33.2 0.6 dynamic-slice.4
  34.4 0.3 concatenate.29
  34.7 0.9 multiply_add_fusion
  35.7 19.0 %all_gather.9 = f32[106,1536]{1,0:T(8,128)} all-gather(f32[106,384]{1,0:T(8,128)S(1)} %get-tuple-element.9), channel_id=1, replica_groups=mesh['dp'=4,'fsdp'=4,'crop'=2] {'fsdp'}, dimensions={1}, use_global_device_ids=true | all-gather | bytes 814080 | tf_op jit(solution)/shard_map/all_gather | solution.py:61
  54.6 0.0 all-gather.6.cloned.1.call-update
  54.7 0.0 all-gather.4.cloned.1.call-start
  54.7 42.3 %all-gather.6.cloned.1.call-done = f32[8,106,1536]{2,1,0:T(8,128)} async-done(((f32[1,106,1536]{2,1,0:T(8,128)}), f32[8,106,1536]{2,1,0:T(8,128)}) %all-gather.6.cloned.1.call-update) | async-done | bytes 5210128 | tf_op jit(solution)/shard_map/all_gather | solution.py:62
  97.0 4.5 %reshape.278 = f32[848,1536]{1,0:T(8,128)} reshape(f32[8,106,1536]{2,1,0:T(8,128)} %all-gather.6.cloned.1.call-done) | data formatting | bytes 10420224
  101.5 1.0 slice_reduce_fusion.1
  102.5 4.9 %fusion.9 = f32[256,1536]{1,0:T(8,128)S(1)} fusion(f32[848,1536]{1,0:T(8,128)} %reshape.278, f32[1536]{0:T(1024)S(1)} %get-tuple-element.8, bf16[1,1,256,588]{2,3,1,0:T(8,128)(2,1)S(1)} %copy-done), kind=kOutput, calls=%fused_computation.5 | convolution fusion | flops 2775318528 | bytes 7090176 | tf_op jit(solution)/shard_map/dot_general | solution.py:44
  107.4 0.3 fusion.15
  107.7 0.5 multiply_reduce_fusion
  108.1 0.4 fusion.14
  108.5 2.8 %copy.14 = f32[1,1,257,1536]{3,0,2,1:T(1,128)} copy(f32[1,1,257,1536]{3,2,1,0:T(8,128)S(1)} %fusion.14) | data formatting | bytes 3158016 | tf_op jit(solution)/shard_map/add | solution.py:53
  111.3 0.0 all-gather.4.cloned.1.call-update
  111.3 12.3 %all-gather.4.cloned.1.call-done = f32[1,2,257,1536]{3,0,2,1:T(1,128)} async-done(((f32[1,1,257,1536]{3,0,2,1:T(1,128)}), f32[1,2,257,1536]{3,0,2,1:T(1,128)}) %all-gather.4.cloned.1.call-update) | async-done | bytes 3158032 | tf_op jit(solution)/shard_map/all_gather | solution.py:64
  123.6 4.0 %fusion.19 = (f32[1,1,257,1536]{3,0,2,1:T(1,128)S(1)}, f32[1,1,257,1536]{3,0,2,1:T(1,128)S(1)}) fusion(f32[1,2,257,1536]{3,0,2,1:T(1,128)} %all-gather.4.cloned.1.call-done), kind=kLoop, calls=%fused_computation.30 | loop fusion | bytes 6316032 | tf_op jit(solution)/shard_map/slice | solution.py:65
  127.7 0.2 copy_bitcast_fusion
  127.9 3.2 %broadcast_select_fusion = f32[1,2,257,1536]{3,1,2,0:T(2,128)} fusion(pred[2]{0:T(512)(128)(4,1)S(1)} %compare_bitcast_fusion, f32[257,1536]{1,0:T(8,128)S(1)} %get-tuple-element.18, f32[257,1536]{1,0:T(8,128)S(1)} %get-tuple-element.19), kind=kLoop, calls=%fused_computation.2 | loop fusion | flops 789504 | bytes 6316034 | tf_op jit(solution)/shard_map/jit(_where)/select_n | solution.py:65
  (19 shorter events, 0.1 us)
Async XLA Ops:
  7.2 95.4 %copy-start = (bf16[1,1,256,588]{2,3,1,0:T(8,128)(2,1)S(1)}, bf16[1,1,256,588]{2,3,1,0:T(8,128)(2,1)}, u32[]{:S(2)}) copy-start(bf16[1,1,256,588]{2,3,1,0:T(8,128)(2,1)} %param.14) | copy-start | bytes 903172
  7.2 26.0 %copy-start.6 = (u32[32]{0:T(128)S(1)}, u32[32]{0:T(128)}, u32[]{:S(2)}) copy-start(u32[32]{0:T(128)} %constant.56) | copy-start | bytes 388
  7.2 27.5 %copy-start.2 = (f32[106,384]{1,0:T(8,128)S(1)}, f32[106,384]{1,0:T(8,128)}, u32[]{:S(2)}) copy-start(f32[106,384]{1,0:T(8,128)} %param.10) | copy-start | bytes 488452
  7.2 27.5 %copy-start.5 = (f32[106,384]{1,0:T(8,128)S(1)}, f32[106,384]{1,0:T(8,128)}, u32[]{:S(2)}) copy-start(f32[106,384]{1,0:T(8,128)} %param.11) | copy-start | bytes 488452
  7.2 27.5 %copy-start.4 = (f32[106,384]{1,0:T(8,128)S(1)}, f32[106,384]{1,0:T(8,128)}, u32[]{:S(2)}) copy-start(f32[106,384]{1,0:T(8,128)} %param.12) | copy-start | bytes 488452
  7.2 27.5 %copy-start.3 = (f32[106,384]{1,0:T(8,128)S(1)}, f32[106,384]{1,0:T(8,128)}, u32[]{:S(2)}) copy-start(f32[106,384]{1,0:T(8,128)} %param.9) | copy-start | bytes 488452
  7.2 89.8 %all-gather.6.cloned.1.call-start = ((), (), s32[]{:S(2)}) async-start(), calls=%async_computation.1 | async-start | bytes 6193152 | tf_op jit(solution)/shard_map/all_gather | solution.py:62
  31.0 3.4 %collective-permute-start = (f32[42,384]{1,0:T(8,128)S(1)}, f32[42,384]{1,0:T(8,128)S(1)}, u32[]{:S(2)}, u32[]{:S(2)}) collective-permute-start(f32[42,384]{1,0:T(8,128)S(1)} %slice.45), channel_id=1, source_target_pairs={{0,1},{1,8},{8,9},{9,16},{16,17},{17,24},{24,25},{2,3},{3,10},{10,... | collective-permute-start | bytes 193544
  35.7 65.8 %copy-start.1 = (f32[106,384]{1,0:T(8,128)}, f32[106,384]{1,0:T(8,128)S(1)}, u32[]{:S(2)}) copy-start(f32[106,384]{1,0:T(8,128)S(1)} %get-tuple-element.9) | copy-start | bytes 488452
  54.7 68.9 %all-gather.4.cloned.1.call-start = ((), (), s32[]{:S(2)}) async-start(), calls=%async_computation | async-start | bytes 4737024 | tf_op jit(solution)/shard_map/all_gather | solution.py:64
  108.5 2.8 %copy-start.7 = (s32[1,2]{1,0:T(1,128)S(1)}, s32[1,2]{1,0:T(1,128)}, u32[]{:S(2)}) copy-start(s32[1,2]{1,0:T(1,128)} %param.15) | copy-start | bytes 28
Sparse Core Ops, SparseCore 0:
  54.8 42.1 all-gather.5
  111.4 12.1 all-gather.3
where the time goes:
time: 138 us
  waiting for transfers between devices  54.6 us (40%)
  blocking collectives  42.7 us (31%)
  between operations  15.7 us (11%)
  local copies, waits for them, and re-layouts  13.4 us (10%)
  other arithmetic  5.28 us (4%)
  matrix products  4.87 us (4%)
    all_gather x1, waiting for transfers between devices, shards(): gathered = lax.all_gather(column_block, ('dp', 'crop'), axis=0, tiled=True)  42.3 us
    unnamed x1, blocking collectives  23.7 us
    all_gather x1, blocking collectives, shards(): column_block = lax.all_gather(teacher_new, 'fsdp', axis=1, tiled=True)  19 us
    all_gather x1, waiting for transfers between devices, shards(): both = lax.all_gather(own_tokens[:, None], 'crop', axis=1, tiled=True)  12.3 us
    unnamed x21, local copies, waits for them, and re-layouts  5.6 us
    dot_general x1, matrix products, embed(): jnp.dot(flat_patches, weight, precision=lax.Precision.HIGHEST, preferred_...  4.87 us
    slice x1, local copies, waits for them, and re-layouts, shards(): both[:, 0:1]  4.05 us
    select_n x1, other arithmetic, shards(): jnp.where((assign == 0)[:, :, None, None], both[:, 0:1], both[:, 1:2])  3.22 us
  transfers between devices with their start and end apart: 3, of which 2 were waited for; matrix products, arithmetic and copies ran while one was open for 0% of the time, Pallas kernels for 0%

commit v1 on v0

--- a/solution.py
+++ b/solution.py
@@ -12,6 +12,18 @@
 momentum_base = 0.992
 plan_length = 625000.0
 norm_epsilon = 1e-06
+
+
+def stops_all_use(s0):
+    return jnp.concatenate(
+        lax.all_to_all(
+            jnp.stack(tuple((s0 for _ in range(lax.psum(1, axis_name="crop")))), axis=0),
+            axis_name="crop",
+            split_axis=0,
+            concat_axis=0,
+        ),
+        1,
+    )
 
 
 def optimize(gradient, student, teacher, moment1, moment2, step_count):
@@ -61,7 +73,7 @@
     column_block = lax.all_gather(teacher_new, "fsdp", axis=1, tiled=True)
     gathered = lax.all_gather(column_block, ("dp", "crop"), axis=0, tiled=True)
     own_tokens = embed(pixels[:, 0], gathered)
-    both = lax.all_gather(own_tokens[:, None], "crop", axis=1, tiled=True)
+    both = stops_all_use(own_tokens[:, None])
     teacher_tokens = jnp.where((assign == 0)[:, :, None, None], both[:, 0:1], both[:, 1:2])
     return (student_new, first_moment, second_moment, teacher_new, update, teacher_tokens)
 

time: 138 us -> 131 us (0.949)
  waiting for transfers between devices: 54.6 us -> 42.4 us
  blocking collectives: 42.7 us -> 48.9 us
  local copies, waits for them, and re-layouts: 13.4 us -> 12 us
    all_gather x1 -> x0, waiting for transfers between devices: 12.3 us -> none  [shards(): both = lax.all_gather(own_tokens[:, None], 'crop', axis=1, tiled=True)]
    all_to_all x0 -> x1, blocking collectives: none -> 6.24 us  [stops_all_use(): lax.all_to_all(jnp.stack(tuple((s0 for _ in range(lax.psum(1, axis_name='...]
    another operation x0 -> x1, local copies, waits for them, and re-layouts: none -> 3.25 us  [stops_all_use(): jnp.stack(tuple((s0 for _ in range(lax.psum(1, axis_name='crop')))), axis=0)]
    add x1 -> x0, local copies, waits for them, and re-layouts: 2.77 us -> none  [embed(): return centered * lax.rsqrt(variance + norm_epsilon) * extras[2] + extras[3]]
    slice x1, local copies, waits for them, and re-layouts: 4.05 us -> 2.16 us  [shards(): both[:, 0:1]]
  transfers between devices with their start and end apart: 3 -> 2, of which waited for: 2 -> 1; matrix products, arithmetic and copies ran while one was open for 0% -> 0% of each run, Pallas kernels for 0% -> 0%
where the time goes in v1:
time: 131 us
  blocking collectives  48.9 us (37%)
  waiting for transfers between devices  42.4 us (32%)
  between operations  15.7 us (12%)
  local copies, waits for them, and re-layouts  12 us (9%)
  other arithmetic  5.67 us (4%)
  matrix products  4.87 us (4%)
  starting transfers between devices  1.33 us (1%)
    all_gather x1, waiting for transfers between devices, shards(): gathered = lax.all_gather(column_block, ('dp', 'crop'), axis=0, tiled=True)  42.3 us
    unnamed x1, blocking collectives  23.7 us
    all_gather x1, blocking collectives, shards(): column_block = lax.all_gather(teacher_new, 'fsdp', axis=1, tiled=True)  19 us
    all_to_all x1, blocking collectives, stops_all_use(): lax.all_to_all(jnp.stack(tuple((s0 for _ in range(lax.psum(1, axis_name='...  6.24 us
    unnamed x21, local copies, waits for them, and re-layouts  5.59 us
    dot_general x1, matrix products, embed(): jnp.dot(flat_patches, weight, precision=lax.Precision.HIGHEST, preferred_...  4.87 us
    another operation x1, local copies, waits for them, and re-layouts, stops_all_use(): jnp.stack(tuple((s0 for _ in range(lax.psum(1, axis_name='crop')))), axis=0)  3.25 us
    select_n x1, other arithmetic, shards(): jnp.where((assign == 0)[:, :, None, None], both[:, 0:1], both[:, 1:2])  3.22 us
  transfers between devices with their start and end apart: 2, of which 1 were waited for; matrix products, arithmetic and copies ran while one was open for 0% of the time, Pallas kernels for 0%

profile of v1, /device:TPU:0, one launch (start us, length us, event | category | flops | bytes accessed | tf_op | source)
XLA Modules:
  0.0 130.9 jit_solution(597426820782526132)
XLA Ops:
  7.2 0.0 copy-start
  7.2 0.0 copy-start.6
  7.2 0.0 all-gather.3.cloned.1.call-start
  7.3 23.7 %fusion = f32[112,384]{1,0:T(8,128)S(1)} fusion(f32[848,384]{1,0:T(8,128)} %bitcast.33), kind=kCustom, calls=%all-reduce-scatter | all-reduce-scatter fusion | flops 344065 | bytes 1475072
  31.0 1.3 collective-permute-start
  33.2 0.6 dynamic-slice.4
  34.4 0.3 concatenate.29
  34.7 0.0 copy-start.7
  34.8 0.9 multiply_add_fusion
  35.7 19.0 %all_gather.6 = f32[106,1536]{1,0:T(8,128)} all-gather(f32[106,384]{1,0:T(8,128)S(1)} %get-tuple-element.9), channel_id=1, replica_groups=mesh['dp'=4,'fsdp'=4,'crop'=2] {'fsdp'}, dimensions={1}, use_global_device_ids=true | all-gather | bytes 814080 | tf_op jit(solution)/shard_map/all_gather | solution.py:73
  54.7 0.0 all-gather.3.cloned.1.call-update
  54.7 42.3 %all-gather.3.cloned.1.call-done = f32[8,106,1536]{2,1,0:T(8,128)} async-done(((f32[1,106,1536]{2,1,0:T(8,128)}), f32[8,106,1536]{2,1,0:T(8,128)}) %all-gather.3.cloned.1.call-update) | async-done | bytes 5210128 | tf_op jit(solution)/shard_map/all_gather | solution.py:74
  97.0 4.5 %reshape.282 = f32[848,1536]{1,0:T(8,128)} reshape(f32[8,106,1536]{2,1,0:T(8,128)} %all-gather.3.cloned.1.call-done) | data formatting | bytes 10420224
  101.5 1.0 slice_reduce_fusion.1
  102.5 4.9 %fusion.9 = f32[256,1536]{1,0:T(8,128)S(1)} fusion(f32[848,1536]{1,0:T(8,128)} %reshape.282, f32[1536]{0:T(1024)S(1)} %get-tuple-element.8, bf16[1,1,256,588]{2,3,1,0:T(8,128)(2,1)S(1)} %copy-done), kind=kOutput, calls=%fused_computation.6 | convolution fusion | flops 2775318528 | bytes 7090176 | tf_op jit(solution)/shard_map/dot_general | solution.py:56
  107.4 0.3 fusion.15
  107.7 0.5 multiply_reduce_fusion
  108.1 0.4 fusion.14
  108.5 0.4 pad_maximum_fusion
  108.9 3.2 %copy.14 = f32[2,1,1,257,1536]{4,2,3,1,0:T(1,128)S(1)} copy(f32[2,1,1,257,1536]{4,3,2,1,0:T(8,128)S(1)} %pad_maximum_fusion) | data formatting | bytes 6316032 | tf_op jit(solution)/shard_map/stack | solution.py:20
  112.2 6.2 %all_to_all.5 = f32[2,1,1,257,1536]{4,2,3,1,0:T(1,128)S(1)} all-to-all(f32[2,1,1,257,1536]{4,2,3,1,0:T(1,128)S(1)} %copy.14), channel_id=1, replica_groups=mesh['dp'=4,'fsdp'=4,'crop'=2] {'crop'}, dimensions={0} | all-to-all | bytes 6316032 | tf_op jit(solution)/shard_map/all_to_all | solution.py:19
  118.4 2.2 %fusion.19 = (f32[1,1,257,1536]{3,0,2,1:T(1,128)S(1)}, f32[1,1,257,1536]{3,0,2,1:T(1,128)S(1)}) fusion(f32[1,2,257,1536]{3,0,2,1:T(1,128)S(1)} %bitcast.31), kind=kLoop, calls=%fused_computation.31 | loop fusion | bytes 6316032 | tf_op jit(solution)/shard_map/slice | solution.py:77
  120.6 0.2 copy_bitcast_fusion
  120.8 3.2 %broadcast_select_fusion = f32[1,2,257,1536]{3,1,2,0:T(2,128)} fusion(pred[2]{0:T(512)(128)(4,1)S(1)} %compare_bitcast_fusion, f32[257,1536]{1,0:T(8,128)S(1)} %get-tuple-element.18, f32[257,1536]{1,0:T(8,128)S(1)} %get-tuple-element.19), kind=kLoop, calls=%fused_computation.3 | loop fusion | flops 789504 | bytes 6316034 | tf_op jit(solution)/shard_map/jit(_where)/select_n | solution.py:77
  (18 shorter events, 0.1 us)
Async XLA Ops:
  7.2 95.4 %copy-start = (bf16[1,1,256,588]{2,3,1,0:T(8,128)(2,1)S(1)}, bf16[1,1,256,588]{2,3,1,0:T(8,128)(2,1)}, u32[]{:S(2)}) copy-start(bf16[1,1,256,588]{2,3,1,0:T(8,128)(2,1)} %param.14) | copy-start | bytes 903172
  7.2 26.0 %copy-start.6 = (u32[32]{0:T(128)S(1)}, u32[32]{0:T(128)}, u32[]{:S(2)}) copy-start(u32[32]{0:T(128)} %constant.56) | copy-start | bytes 388
  7.2 27.5 %copy-start.2 = (f32[106,384]{1,0:T(8,128)S(1)}, f32[106,384]{1,0:T(8,128)}, u32[]{:S(2)}) copy-start(f32[106,384]{1,0:T(8,128)} %param.10) | copy-start | bytes 488452
  7.2 27.5 %copy-start.5 = (f32[106,384]{1,0:T(8,128)S(1)}, f32[106,384]{1,0:T(8,128)}, u32[]{:S(2)}) copy-start(f32[106,384]{1,0:T(8,128)} %param.11) | copy-start | bytes 488452
  7.2 27.5 %copy-start.4 = (f32[106,384]{1,0:T(8,128)S(1)}, f32[106,384]{1,0:T(8,128)}, u32[]{:S(2)}) copy-start(f32[106,384]{1,0:T(8,128)} %param.12) | copy-start | bytes 488452
  7.2 27.5 %copy-start.3 = (f32[106,384]{1,0:T(8,128)S(1)}, f32[106,384]{1,0:T(8,128)}, u32[]{:S(2)}) copy-start(f32[106,384]{1,0:T(8,128)} %param.9) | copy-start | bytes 488452
  7.2 89.8 %all-gather.3.cloned.1.call-start = ((), (), s32[]{:S(2)}) async-start(), calls=%async_computation.1 | async-start | bytes 6193152 | tf_op jit(solution)/shard_map/all_gather | solution.py:74
  31.0 3.4 %collective-permute-start = (f32[42,384]{1,0:T(8,128)S(1)}, f32[42,384]{1,0:T(8,128)S(1)}, u32[]{:S(2)}, u32[]{:S(2)}) collective-permute-start(f32[42,384]{1,0:T(8,128)S(1)} %slice.45), channel_id=1, source_target_pairs={{0,1},{1,8},{8,9},{9,16},{16,17},{17,24},{24,25},{2,3},{3,10},{10,... | collective-permute-start | bytes 193544
  34.7 19.9 %copy-start.7 = (s32[1,2]{1,0:T(1,128)S(1)}, s32[1,2]{1,0:T(1,128)}, u32[]{:S(2)}) copy-start(s32[1,2]{1,0:T(1,128)} %param.15) | copy-start | bytes 28
  35.7 65.8 %copy-start.1 = (f32[106,384]{1,0:T(8,128)}, f32[106,384]{1,0:T(8,128)S(1)}, u32[]{:S(2)}) copy-start(f32[106,384]{1,0:T(8,128)S(1)} %get-tuple-element.9) | copy-start | bytes 488452
Sparse Core Ops, SparseCore 0:
  54.8 42.1 all-gather.2
